TPU v7x, 32 devices: a whole 2x2x4 slice. The times are simulated.
32 devices in a mesh: dp: 8 (over z, y), tp: 4 (over x, core).
Axes of the slice: x: 2, y: 2, z: 4, core: 2. Of those that a mesh axis runs over, the one named last changes fastest.
Arguments:
- tokens: bfloat16 [32, 1024, 768], P(('dp', 'tp')), may hold values from -11 to 11
- clip_lengths: int32 [32, 4], P(('dp', 'tp')), may hold values from 1 to 384, as said below
- out_grad: bfloat16 [32, 1024, 768], P(('dp', 'tp')), may hold values from -6 to 6
- w_query: bfloat16 [768, 768], P(('dp', 'tp')), may hold values from -0.21875 to 0.21875
- w_key: bfloat16 [768, 768], P(('dp', 'tp')), may hold values from -0.21875 to 0.21875
- w_value: bfloat16 [768, 768], P(('dp', 'tp')), may hold values from -0.21875 to 0.21875
- w_output: bfloat16 [768, 768], P(('dp', 'tp')), may hold values from -2.5 to 2.5
- gain_attention: bfloat16 [768], P(('dp', 'tp')), may hold values from 0.099609375 to 1.8984375
- gain_feed: bfloat16 [768], P(('dp', 'tp')), may hold values from 0.099609375 to 1.8984375
- w_expand: bfloat16 [768, 3072], P('dp', 'tp'), may hold values from -0.21875 to 0.21875
- w_reduce: bfloat16 [3072, 768], P('tp', 'dp'), may hold values from -0.4375 to 0.4375
Outputs:
- block_out: bfloat16 [32, 1024, 768], P(('dp', 'tp'))
- grad_tokens: float32 [32, 1024, 768], P(('dp', 'tp'))
- grad_w_query: float32 [768, 768], P(('dp', 'tp'))
- grad_w_key: float32 [768, 768], P(('dp', 'tp'))
- grad_w_value: float32 [768, 768], P(('dp', 'tp'))
- grad_w_output: float32 [768, 768], P(('dp', 'tp'))
- grad_gain_attention: float32 [768], P(('dp', 'tp'))
- grad_gain_feed: float32 [768], P(('dp', 'tp'))
- grad_w_expand: float32 [768, 3072], P('dp', 'tp')
- grad_w_reduce: float32 [3072, 768], P('tp', 'dp')
- root_mean_squares: float32 [3], replicated
Inputs may be any that keep to these rules, and one draw needn't show every extreme that they name: Each row of clip_lengths gives the lengths of its 3 clips in order, each at most 384 with one of exactly 384 in every row, then the number of padding slots at the row's end, 1 to 256; a row's entries sum to 1024.
All inputs are finite; a program needn't handle non-finite values.
Results may differ from a plain program's by a relative error of at most 0.015.
Values may be sent and summed in bfloat16 or wider, within the bound.
A program may use at most 192 MiB of HBM per device.

v0:
```python
from functools import partial

import jax
import jax.numpy as jnp
from jax import lax
from jax.sharding import PartitionSpec as P

HEADS = 12
HEAD_DIM = 64
SLOTS = 4


def segment_numbers(lengths, pack_len):
    clip_ends = jnp.cumsum(lengths[:, :-1], axis=-1, dtype=jnp.int32)
    position = jnp.arange(pack_len, dtype=jnp.int32)
    return jnp.sum(
        (position[None, :, None] >= clip_ends[:, None, :]).astype(jnp.int32),
        axis=-1,
        dtype=jnp.int32,
    )


def normalize(array_in):
    average = jnp.mean(array_in, axis=-1, keepdims=True)
    centred = array_in - average
    spread = jnp.mean(centred * centred, axis=-1, keepdims=True)
    inv_scale = lax.rsqrt(spread + 1e-06)
    return (centred * inv_scale, inv_scale)


def norm_back(grad_normed, unit_value, inv_scale, gain_vec):
    scaled = grad_normed * gain_vec
    inner_sum = (
        scaled
        - jnp.mean(scaled, axis=-1, keepdims=True)
        - unit_value * jnp.mean(scaled * unit_value, axis=-1, keepdims=True)
    )
    return (inv_scale * inner_sum, jnp.sum(grad_normed * unit_value, axis=0))


def dot_plain(left_side, right_side):
    return jnp.dot(left_side, right_side, preferred_element_type=jnp.float32)


def dot_first(left_side, right_side):
    return lax.dot_general(
        left_side, right_side, (((0,), (0,)), ((), ())), preferred_element_type=jnp.float32
    )


def dot_last(left_side, right_side):
    return lax.dot_general(
        left_side, right_side, (((1,), (1,)), ((), ())), preferred_element_type=jnp.float32
    )


def split_heads(array_in, rows_dev, pack_len):
    return (
        array_in.reshape(rows_dev, pack_len, HEADS, HEAD_DIM)
        .transpose(0, 2, 1, 3)
        .reshape(rows_dev * HEADS, pack_len, HEAD_DIM)
    )


def merge_heads(array_in, rows_dev, pack_len):
    return (
        array_in.reshape(rows_dev, HEADS, pack_len, HEAD_DIM)
        .transpose(0, 2, 1, 3)
        .reshape(rows_dev * pack_len, HEADS * HEAD_DIM)
    )


def head_scores(query_head, key_head, segments):
    same_clip = segments[:, None] == segments[None, :]
    scores = dot_last(query_head, key_head) * 0.125
    return jnp.where(same_clip, scores, -1e30)


def head_forward(block_item):
    query_head, key_head, value_head, segments = block_item
    scores = head_scores(query_head, key_head, segments)
    row_max = jnp.max(scores, axis=-1, keepdims=True)
    exponent = jnp.exp(scores - row_max)
    row_sum = jnp.sum(exponent, axis=-1, keepdims=True)
    weights = (exponent / row_sum).astype(jnp.bfloat16)
    return (dot_plain(weights, value_head).astype(jnp.bfloat16), row_max, row_sum)


def head_backward(block_item):
    query_head, key_head, value_head, segments, row_max, row_sum, grad_head = block_item
    scores = head_scores(query_head, key_head, segments)
    probabilities = jnp.exp(scores - row_max) / row_sum
    grad_probs = dot_last(grad_head, value_head)
    grad_value = dot_first(probabilities.astype(jnp.bfloat16), grad_head)
    inner_sum = jnp.sum(probabilities * grad_probs, axis=-1, keepdims=True)
    grad_scores = (probabilities * (grad_probs - inner_sum)).astype(jnp.bfloat16)
    grad_query = (dot_plain(grad_scores, key_head) * 0.125).astype(jnp.bfloat16)
    grad_key = (dot_first(grad_scores, query_head) * 0.125).astype(jnp.bfloat16)
    return (grad_query, grad_key, grad_value.astype(jnp.bfloat16))


def on_device(
    tokens,
    clip_lengths,
    out_grad,
    w_query,
    w_key,
    w_value,
    w_output,
    gain_attention,
    gain_feed,
    w_expand,
    w_reduce,
):
    rows_dev, pack_len, width = tokens.shape
    token_count = rows_dev * pack_len
    segments = segment_numbers(clip_lengths, pack_len)
    valid_rows = (segments < SLOTS - 1).astype(jnp.float32).reshape(-1)
    valid_column = valid_rows[:, None]
    inputs = tokens.reshape(token_count, width).astype(jnp.float32)
    query_full, key_full, value_full, output_full, gain_one, gain_two = (
        lax.all_gather(w_query, ("dp", "tp"), axis=0, tiled=True),
        lax.all_gather(w_key, ("dp", "tp"), axis=0, tiled=True),
        lax.all_gather(w_value, ("dp", "tp"), axis=0, tiled=True),
        lax.all_gather(w_output, ("dp", "tp"), axis=0, tiled=True),
        lax.all_gather(gain_attention, ("dp", "tp"), axis=0, tiled=True),
        lax.all_gather(gain_feed, ("dp", "tp"), axis=0, tiled=True),
    )
    expand_full, reduce_full = (
        lax.all_gather(w_expand, "dp", axis=0, tiled=True),
        lax.all_gather(w_reduce, "dp", axis=1, tiled=True),
    )
    gain_one = gain_one.astype(jnp.float32)
    gain_two = gain_two.astype(jnp.float32)
    unit_one, scale_one = normalize(inputs)
    normed = (unit_one * gain_one).astype(jnp.bfloat16)
    query_rows = dot_plain(normed, query_full).astype(jnp.bfloat16)
    key_rows = dot_plain(normed, key_full).astype(jnp.bfloat16)
    value_rows = dot_plain(normed, value_full).astype(jnp.bfloat16)
    head_segments = jnp.repeat(segments, HEADS, axis=0)
    query_heads = split_heads(query_rows, rows_dev, pack_len)
    key_heads = split_heads(key_rows, rows_dev, pack_len)
    value_heads = split_heads(value_rows, rows_dev, pack_len)
    mixed_heads, row_maxima, row_sums = lax.map(
        head_forward, (query_heads, key_heads, value_heads, head_segments)
    )
    mixed_rows = merge_heads(mixed_heads, rows_dev, pack_len)
    branch = dot_plain(mixed_rows, output_full)
    middle = inputs + branch
    unit_two, scale_two = normalize(middle)
    normed_feed = (unit_two * gain_two).astype(jnp.bfloat16)
    normed_rows = lax.all_gather(normed_feed, "tp", axis=0, tiled=True)
    hidden = dot_plain(normed_rows, expand_full)
    gelu_value, gelu_pull = jax.vjp(partial(jax.nn.gelu, approximate=False), hidden)
    active = gelu_value.astype(jnp.bfloat16)
    feed_out = lax.psum_scatter(
        dot_plain(
            lax.slice_in_dim(active, 0, token_count * lax.axis_size("tp"), axis=0), reduce_full
        ),
        "tp",
        scatter_dimension=0,
        tiled=True,
    )
    result = (middle + feed_out).astype(jnp.bfloat16).reshape(rows_dev, pack_len, width)
    totals_all = lax.psum(
        (
            jnp.sum(inputs * inputs * valid_column),
            jnp.sum(branch * branch * valid_column),
            jnp.sum(feed_out * feed_out * valid_column),
            jnp.sum(valid_rows),
        ),
        ("dp", "tp"),
    )
    rms_stats = jnp.sqrt(jnp.stack(totals_all[:3]) / (totals_all[3] * width))
    grad_result = out_grad.reshape(token_count, width).astype(jnp.float32) * valid_column
    grad_feed = grad_result.astype(jnp.bfloat16)
    grad_rows = lax.all_gather(grad_feed, "tp", axis=0, tiled=True)
    grad_reduce = dot_first(active, grad_rows)
    grad_active = dot_last(grad_rows, reduce_full)
    grad_hidden = gelu_pull(grad_active)[0].astype(jnp.bfloat16)
    grad_expand = dot_first(normed_rows, grad_hidden)
    grad_normed_feed = lax.psum_scatter(
        dot_last(grad_hidden, expand_full), "tp", scatter_dimension=0, tiled=True
    )
    grad_norm_two, grad_gain_two = norm_back(grad_normed_feed, unit_two, scale_two, gain_two)
    grad_middle = grad_result + grad_norm_two
    grad_branch = grad_middle.astype(jnp.bfloat16)
    grad_output_w = dot_first(mixed_rows, grad_branch)
    grad_mixed = dot_last(grad_branch, output_full).astype(jnp.bfloat16)
    grad_heads = split_heads(grad_mixed, rows_dev, pack_len)
    grad_query_heads, grad_key_heads, grad_value_heads = lax.map(
        head_backward,
        (query_heads, key_heads, value_heads, head_segments, row_maxima, row_sums, grad_heads),
    )
    grad_query = merge_heads(grad_query_heads, rows_dev, pack_len)
    grad_key = merge_heads(grad_key_heads, rows_dev, pack_len)
    grad_value = merge_heads(grad_value_heads, rows_dev, pack_len)
    grad_query_w = dot_first(normed, grad_query)
    grad_key_w = dot_first(normed, grad_key)
    grad_value_w = dot_first(normed, grad_value)
    grad_normed = (
        dot_last(grad_query, query_full)
        + dot_last(grad_key, key_full)
        + dot_last(grad_value, value_full)
    )
    grad_norm_one, grad_gain_one = norm_back(grad_normed, unit_one, scale_one, gain_one)
    grad_inputs = (grad_middle + grad_norm_one).reshape(rows_dev, pack_len, width)
    shard_expand, shard_reduce = (
        lax.psum_scatter(grad_expand, "dp", scatter_dimension=0, tiled=True),
        lax.psum_scatter(grad_reduce, "dp", scatter_dimension=1, tiled=True),
    )
    shard_query, shard_key, shard_value, shard_output, shard_gain_one, shard_gain_two = (
        lax.psum_scatter(grad_query_w, ("dp", "tp"), scatter_dimension=0, tiled=True),
        lax.psum_scatter(grad_key_w, ("dp", "tp"), scatter_dimension=0, tiled=True),
        lax.psum_scatter(grad_value_w, ("dp", "tp"), scatter_dimension=0, tiled=True),
        lax.psum_scatter(grad_output_w, ("dp", "tp"), scatter_dimension=0, tiled=True),
        lax.psum_scatter(grad_gain_one, ("dp", "tp"), scatter_dimension=0, tiled=True),
        lax.psum_scatter(grad_gain_two, ("dp", "tp"), scatter_dimension=0, tiled=True),
    )
    return (
        result,
        grad_inputs,
        shard_query,
        shard_key,
        shard_value,
        shard_output,
        shard_gain_one,
        shard_gain_two,
        shard_expand,
        shard_reduce,
        rms_stats,
    )


def solution(mesh):
    in_specs = (
        P(("dp", "tp"), None, None),
        P(("dp", "tp"), None),
        P(("dp", "tp"), None, None),
        P(("dp", "tp"), None),
        P(("dp", "tp"), None),
        P(("dp", "tp"), None),
        P(("dp", "tp"), None),
        P(("dp", "tp")),
        P(("dp", "tp")),
        P("dp", "tp"),
        P("tp", "dp"),
    )
    out_specs = (
        P(("dp", "tp"), None, None),
        P(("dp", "tp"), None, None),
        P(("dp", "tp"), None),
        P(("dp", "tp"), None),
        P(("dp", "tp"), None),
        P(("dp", "tp"), None),
        P(("dp", "tp")),
        P(("dp", "tp")),
        P("dp", "tp"),
        P("tp", "dp"),
        P(),
    )
    return jax.shard_map(
        on_device, mesh=mesh, in_specs=in_specs, out_specs=out_specs, check_vma=False
    )
```

profile of v0, /device:TPU:0, one launch (start us, length us, event | category | flops | bytes accessed | tf_op | source)
XLA Modules:
  0.0 1258.6 jit_solution(7682637012286789652)
XLA Ops:
  13.2 42.1 %all-reduce.5 = (bf16[768]{0:T(1024)(128)(2,1)S(1)}, bf16[768]{0:T(1024)(128)(2,1)S(1)}) all-reduce(bf16[768]{0:T(1024)(128)(2,1)S(1)} %dynamic-update-slice, bf16[768]{0:T(1024)(128)(2,1)S(1)} %dynamic-update-slice.1), channel_id=1, replica_groups=mesh['dp'=8,'tp'=4] {'dp','tp'}, use_global_device_ids=true, to_apply=%add | all-reduce | flops 1536 | bytes 6144
  56.0 11.7 all-gather.9.cloned.1.call-done
  73.3 50.4 %all-gather.11.cloned.1.call-done = bf16[768,768]{1,0:T(8,128)(2,1)} async-done(((bf16[24,768]{1,0:T(8,128)(2,1)}), bf16[768,768]{1,0:T(8,128)(2,1)}) %all-gather.11.cloned.1.call-update) | async-done | bytes 1179664 | tf_op jit(solution)/shard_map/all_gather | solution.py:123
  129.2 50.3 %all-gather.13.cloned.1.call-done = bf16[768,768]{1,0:T(8,128)(2,1)} async-done(((bf16[24,768]{1,0:T(8,128)(2,1)}), bf16[768,768]{1,0:T(8,128)(2,1)}) %all-gather.13.cloned.1.call-update) | async-done | bytes 1179664 | tf_op jit(solution)/shard_map/all_gather | solution.py:124
  185.4 69.0 %while.28 = (s32[]{:T(128)}, bf16[12,1024,64]{1,2,0:T(8,128)(2,1)S(1)}, f32[12,1024,1]{1,2,0:T(1,128)}, f32[12,1024,1]{1,2,0:T(1,128)}, s32[12,1024]{1,0:T(8,128...) while((s32[]{:T(128)}, ...), condition=%wide.region_7.8_spmd, body=%wide.region_4.7_spmd.sunk | while | flops 284227584 | bytes 13568109 | solution.py:144
  254.5 5.0 fusion.102
  266.0 11.4 all-gather.19.cloned.1.call-done
  277.4 47.2 %all-gather.17.cloned.1.call-done = bf16[4096,768]{0,1:T(8,128)(2,1)} async-done(((bf16[1024,768]{0,1:T(8,128)(2,1)}), bf16[4096,768]{0,1:T(8,128)(2,1)}) %all-gather.17.cloned.1.call-update) | async-done | bytes 6291472 | tf_op jit(solution)/shard_map/all_gather | solution.py:152
  324.5 10.2 fusion.104
  334.7 33.1 %all-gather.21.cloned.1.call-done = bf16[768,768]{0,1:T(8,128)(2,1)} async-done(((bf16[768,96]{0,1:T(8,128)(2,1)}), bf16[768,768]{0,1:T(8,128)(2,1)}) %all-gather.21.cloned.1.call-update) | async-done | bytes 1179664 | tf_op jit(solution)/shard_map/all_gather | solution.py:131
  367.8 46.7 %all-gather.23.cloned.1.call-done = bf16[4096,768]{0,1:T(8,128)(2,1)} async-done(((bf16[1024,768]{0,1:T(8,128)(2,1)}), bf16[4096,768]{0,1:T(8,128)(2,1)}) %all-gather.23.cloned.1.call-update) | async-done | bytes 6291472 | tf_op jit(solution)/shard_map/all_gather | solution.py:177
  414.6 36.4 %add_convert_fusion = (bf16[4096,768]{1,0:T(8,128)(2,1)S(1)}, f32[4096,768]{1,0:T(8,128)}) fusion(f32[4096,768]{1,0:T(8,128)} %fusion.104, bf16[4096,768]{0,1:T(8,128)(2,1)} %all-gather.23.cloned.1.call-done, bf16[768,768]{0,1:T(8,128)(2,1)} %all-gather.21.cloned.1.call-done), kind=kOutput, calls=%fused_computation.64 | convolution fusion | flops 5058330624 | bytes 38928384 | tf_op jit(solution)/shard_map/dot_general | solution.py:52
  453.5 8.0 fusion.106
  461.6 11.3 multiply_convert_fusion.1
  472.9 3.7 copy-done.10
  476.6 7.9 fusion.105
  484.6 10.1 fusion.107
  494.9 10.1 fusion.110
  505.1 55.6 %reduce-scatter.11.cloned.1.call-done = f32[1024,768]{0,1:T(8,128)} async-done(((f32[4096,768]{0,1:T(8,128)}), f32[1024,768]{0,1:T(8,128)}) %reduce-scatter.11.cloned.1.call-update) | async-done | bytes 3145744 | tf_op jit(solution)/shard_map/reduce_scatter | solution.py:182
  563.6 98.6 %reduce-scatter.9.cloned.1.call-done = f32[1024,768]{0,1:T(8,128)} async-done(((f32[4096,768]{0,1:T(8,128)}), f32[1024,768]{0,1:T(8,128)}) %reduce-scatter.9.cloned.1.call-update) | async-done | bytes 3145744 | tf_op jit(solution)/shard_map/reduce_scatter | solution.py:156
  662.2 6.7 multiply_reduce_fusion.2
  676.3 160.4 %while.29 = (s32[]{:T(128)}, bf16[12,1024,64]{1,2,0:T(8,128)(2,1)S(1)}, bf16[12,1024,64]{1,2,0:T(8,128)(2,1)}, bf16[12,1024,64]{1,2,0:T(8,128)(2,1)}, s32[12,102...) while((s32[]{:T(128)}, ...), condition=%wide.region_16.17_spmd, body=%wide.region_14.16_spmd.sunk | while | flops 682949632 | bytes 33739908 | solution.py:191
  839.7 4.3 fusion.94
  844.1 4.5 fusion.92
  848.7 4.8 fusion.86
  856.6 3.3 fusion.108
  867.3 3.6 copy.51
  870.9 39.7 %all-reduce.4 = (f32[768]{0:T(1024)S(1)}, f32[768]{0:T(1024)S(1)}, f32[1]{0:T(128)}, f32[1]{0:T(128)}, f32[1]{0:T(128)}, /*index=5*/f32[]{:T(128)}) all-reduce(f32[768]{0:T(1024)S(1)} %get-tuple-element.155, f32[768]{0:T(1024)S(1)} %get-tuple-element.153, f32[1]{0:T(128)} %bitcast.60, ...), channel_id=8, replica_groups=mesh['dp'=8,'tp'=4] {'dp','tp'}, use_global_device_ids=true, to_apply=%region_24.25.clone | all-reduce | flops 1540 | bytes 12320
  914.8 24.0 %reduce-scatter.13.cloned.1.call-done = f32[24,768]{1,0:T(8,128)} async-done(((f32[768,768]{1,0:T(8,128)}), f32[24,768]{1,0:T(8,128)}) %reduce-scatter.13.cloned.1.call-update) | async-done | bytes 73744 | tf_op jit(solution)/shard_map/reduce_scatter | solution.py:213
  938.8 104.6 %reduce-scatter.15.cloned.1.call-done = f32[24,768]{1,0:T(8,128)} async-done(((f32[768,768]{1,0:T(8,128)}), f32[24,768]{1,0:T(8,128)}) %reduce-scatter.15.cloned.1.call-update) | async-done | bytes 73744 | tf_op jit(solution)/shard_map/reduce_scatter | solution.py:214
  1043.5 103.8 %reduce-scatter.17.cloned.1.call-done = f32[24,768]{1,0:T(8,128)} async-done(((f32[768,768]{1,0:T(8,128)}), f32[24,768]{1,0:T(8,128)}) %reduce-scatter.17.cloned.1.call-update) | async-done | bytes 73744 | tf_op jit(solution)/shard_map/reduce_scatter | solution.py:215
  1147.2 104.6 %reduce-scatter.19.cloned.1.call-done = f32[24,768]{1,0:T(8,128)} async-done(((f32[768,768]{1,0:T(8,128)}), f32[24,768]{1,0:T(8,128)}) %reduce-scatter.19.cloned.1.call-update) | async-done | bytes 73744 | tf_op jit(solution)/shard_map/reduce_scatter | solution.py:216
  (320 shorter events, 288.7 us)
Async XLA Ops:
  7.2 60.6 %all-gather.9.cloned.1.call-start = ((), (), s32[]{:S(2)}) async-start(), calls=%async_computation.8 | async-start | bytes 1216512 | tf_op jit(solution)/shard_map/all_gather | solution.py:122
  7.9 115.7 %all-gather.11.cloned.1.call-start = ((), (), s32[]{:S(2)}) async-start(), calls=%async_computation.9 | async-start | bytes 1216512 | tf_op jit(solution)/shard_map/all_gather | solution.py:123
  8.7 170.9 %all-gather.13.cloned.1.call-start = ((), (), s32[]{:S(2)}) async-start(), calls=%async_computation.10 | async-start | bytes 1216512 | tf_op jit(solution)/shard_map/all_gather | solution.py:124
  9.4 245.0 %all-gather.15.cloned.1.call-start = ((), (), s32[]{:S(2)}) async-start(), calls=%async_computation.11 | async-start | bytes 1216512 | tf_op jit(solution)/shard_map/all_gather | solution.py:125
  10.0 267.4 %all-gather.19.cloned.1.call-start = ((), (), s32[]{:S(2)}) async-start(), calls=%async_computation.13 | async-start | bytes 1327104 | tf_op jit(solution)/shard_map/all_gather | solution.py:130
  10.6 313.9 %all-gather.17.cloned.1.call-start = ((), (), s32[]{:S(2)}) async-start(), calls=%async_computation.12 | async-start | bytes 7864320 | tf_op jit(solution)/shard_map/all_gather | solution.py:152
  12.4 242.1 %copy-start.2 = (bf16[1,1024,768]{1,2,0:T(8,128)(2,1)}, bf16[1,1024,768]{1,2,0:T(8,128)(2,1)S(1)}, u32[]{:S(2)}) copy-start(bf16[1,1024,768]{1,2,0:T(8,128)(2,1)S(1)} %copy.42) | copy-start | bytes 4718596
  12.7 251.6 %copy-start.19 = (s32[1024]{0:T(1024)}, s32[1024]{0:T(1024)S(1)}, u32[]{:S(2)}) copy-start(s32[1024]{0:T(1024)S(1)} %fusion.89) | copy-start | bytes 12292
  55.2 124.3 %copy-start.29 = (f32[768]{0:T(1024)}, f32[768]{0:T(1024)S(1)}, u32[]{:S(2)}) copy-start(f32[768]{0:T(1024)S(1)} %convert_element_type.106) | copy-start | bytes 9220
  55.5 124.0 %copy-start.25 = (f32[1024]{0:T(1024)}, f32[1024]{0:T(1024)S(1)}, u32[]{:S(2)}) copy-start(f32[1024]{0:T(1024)S(1)} %broadcast_multiply_fusion.5) | copy-start | bytes 12292
  56.0 123.6 %copy-start.31 = (f32[1024]{0:T(1024)}, f32[1024]{0:T(1024)S(1)}, u32[]{:S(2)}) copy-start(f32[1024]{0:T(1024)S(1)} %add_rsqrt_fusion.1) | copy-start | bytes 12292
  56.0 203.8 %copy-start.21 = (f32[768]{0:T(1024)}, f32[768]{0:T(1024)S(1)}, u32[]{:S(2)}) copy-start(f32[768]{0:T(1024)S(1)} %convert_element_type.111) | copy-start | bytes 9220
  262.7 105.2 %all-gather.21.cloned.1.call-start = ((), (), s32[]{:S(2)}) async-start(), calls=%async_computation.14 | async-start | bytes 1327104 | tf_op jit(solution)/shard_map/all_gather | solution.py:131
  263.4 151.1 %all-gather.23.cloned.1.call-start = ((), (), s32[]{:S(2)}) async-start(), calls=%async_computation.16 | async-start | bytes 7864320 | tf_op jit(solution)/shard_map/all_gather | solution.py:177
  264.2 70.5 %copy-start.4 = (bf16[1,1024,768]{1,2,0:T(8,128)(2,1)}, bf16[1,1024,768]{1,2,0:T(8,128)(2,1)S(1)}, u32[]{:S(2)}) copy-start(bf16[1,1024,768]{1,2,0:T(8,128)(2,1)S(1)} %copy.47) | copy-start | bytes 4718596
  264.3 70.5 %copy-start.27 = (f32[1024]{0:T(1024)}, f32[1024]{0:T(1024)S(1)}, u32[]{:S(2)}) copy-start(f32[1024]{0:T(1024)S(1)} %compare_convert_fusion.1) | copy-start | bytes 12292
  265.9 294.8 %reduce-scatter.11.cloned.1.call-start = ((), (), s32[]{:S(2)}) async-start(), calls=%async_computation.17 | async-start | bytes 15728640 | tf_op jit(solution)/shard_map/reduce_scatter | solution.py:182
  334.7 118.8 %copy-start.35 = (bf16[768,768]{1,0:T(8,128)(2,1)S(1)}, bf16[768,768]{1,0:T(8,128)(2,1)}, u32[]{:S(2)}) copy-start(bf16[768,768]{1,0:T(8,128)(2,1)} %all-gather.19.cloned.1.call-done) | copy-start | bytes 3538948
  461.5 200.7 %reduce-scatter.9.cloned.1.call-start = ((), (), s32[]{:S(2)}) async-start(), calls=%async_computation.15 | async-start | bytes 15728640 | tf_op jit(solution)/shard_map/reduce_scatter | solution.py:156
  484.6 430.2 %reduce-scatter.21.cloned.1.call-start = ((), (), s32[]{:S(2)}) async-start(), calls=%async_computation.22 | async-start | bytes 2654208 | tf_op jit(solution)/shard_map/reduce_scatter | solution.py:209
  494.8 65.9 %copy-start.18 = (f32[1024]{0:T(1024)S(1)}, f32[1024]{0:T(1024)}, u32[]{:S(2)}) copy-start(f32[1024]{0:T(1024)} %copy-done.17) | copy-start | bytes 12292
  494.8 65.9 %copy-start.22 = (f32[768]{0:T(1024)S(1)}, f32[768]{0:T(1024)}, u32[]{:S(2)}) copy-start(f32[768]{0:T(1024)} %copy-done.21) | copy-start | bytes 9220
  494.8 420.0 %reduce-scatter.23.cloned.1.call-start = ((), (), s32[]{:S(2)}) async-start(), calls=%async_computation.23 | async-start | bytes 2654208 | tf_op jit(solution)/shard_map/reduce_scatter | solution.py:210
  505.0 157.2 %copy-start.28 = (f32[1024]{0:T(1024)S(1)}, f32[1024]{0:T(1024)}, u32[]{:S(2)}) copy-start(f32[1024]{0:T(1024)} %copy-done.27) | copy-start | bytes 12292
  505.1 433.8 %reduce-scatter.13.cloned.1.call-start = ((), (), s32[]{:S(2)}) async-start(), calls=%async_computation.18 | async-start | bytes 2433024 | tf_op jit(solution)/shard_map/reduce_scatter | solution.py:213
  676.3 160.5 %copy-start.3 = (bf16[1,1024,768]{1,2,0:T(8,128)(2,1)S(1)}, bf16[1,1024,768]{1,2,0:T(8,128)(2,1)}, u32[]{:S(2)}) copy-start(bf16[1,1024,768]{1,2,0:T(8,128)(2,1)} %copy-done.2) | copy-start | bytes 4718596
  676.3 160.5 %copy-start.26 = (f32[1024]{0:T(1024)S(1)}, f32[1024]{0:T(1024)}, u32[]{:S(2)}) copy-start(f32[1024]{0:T(1024)} %copy-done.25) | copy-start | bytes 12292
  676.3 160.5 %copy-start.30 = (f32[768]{0:T(1024)S(1)}, f32[768]{0:T(1024)}, u32[]{:S(2)}) copy-start(f32[768]{0:T(1024)} %copy-done.29) | copy-start | bytes 9220
  676.3 160.5 %copy-start.32 = (f32[1024]{0:T(1024)S(1)}, f32[1024]{0:T(1024)}, u32[]{:S(2)}) copy-start(f32[1024]{0:T(1024)} %copy-done.31) | copy-start | bytes 12292
  839.6 203.8 %reduce-scatter.15.cloned.1.call-start = ((), (), s32[]{:S(2)}) async-start(), calls=%async_computation.19 | async-start | bytes 2433024 | tf_op jit(solution)/shard_map/reduce_scatter | solution.py:214
  844.0 303.2 %reduce-scatter.17.cloned.1.call-start = ((), (), s32[]{:S(2)}) async-start(), calls=%async_computation.20 | async-start | bytes 2433024 | tf_op jit(solution)/shard_map/reduce_scatter | solution.py:215
  848.6 403.2 %reduce-scatter.19.cloned.1.call-start = ((), (), s32[]{:S(2)}) async-start(), calls=%async_computation.21 | async-start | bytes 2433024 | tf_op jit(solution)/shard_map/reduce_scatter | solution.py:216
  (25 other events, 221.9 us)
Sparse Core Ops, SparseCore 0:
  10.9 56.7 all-gather.8
  70.7 52.9 all-gather.10
  126.6 52.9 all-gather.12
  182.3 52.9 all-gather.14
  237.4 39.9 all-gather.18
  279.4 45.1 all-gather.16
  326.7 41.0 all-gather.20
  369.4 45.1 all-gather.22
  461.6 99.0 reduce-scatter.10
  563.2 99.0 reduce-scatter.8
  666.3 69.0 reduce-scatter.20
  739.3 67.9 reduce-scatter.22
  839.8 99.0 reduce-scatter.12
  945.4 98.0 reduce-scatter.14
  1049.2 97.9 reduce-scatter.16
  1153.8 97.9 reduce-scatter.18
where the time goes:
time: 1270 us; the launch traced here: 1260 us
  waiting for transfers between devices  746 us (59%)
  matrix products  299 us (24%)
  blocking collectives  81.8 us (6%)
  local copies, waits for them, and re-layouts  57.7 us (5%)
  other arithmetic  57.1 us (4%)
  between operations  15.3 us (1%)
    dot_general x42, matrix products, dot_last(): lax.dot_general(left_side, right_side, (((1,), (1,)), ((), ())), preferre...  128 us
    reduce_scatter x1, waiting for transfers between devices, on_device(): lax.psum_scatter(grad_key_w, ('dp', 'tp'), scatter_dimension=0, tiled=True)  105 us
    reduce_scatter x1, waiting for transfers between devices, on_device(): lax.psum_scatter(grad_output_w, ('dp', 'tp'), scatter_dimension=0, tiled=...  105 us
    reduce_scatter x1, waiting for transfers between devices, on_device(): lax.psum_scatter(grad_value_w, ('dp', 'tp'), scatter_dimension=0, tiled=T...  104 us
    reduce_scatter x1, waiting for transfers between devices, on_device(): lax.psum_scatter(dot_plain(lax.slice_in_dim(active, 0, token_count * lax....  98.6 us
    dot_general x30, matrix products, dot_first(): lax.dot_general(left_side, right_side, (((0,), (0,)), ((), ())), preferre...  93.8 us
    unnamed x2, blocking collectives  81.8 us
    dot_general x30, matrix products, dot_plain(): return jnp.dot(left_side, right_side, preferred_element_type=jnp.float32)  76.9 us
  transfers between devices with their start and end apart: 16, of which 13 were waited for; matrix products, arithmetic and copies ran while one was open for 29% of the time, Pallas kernels for 0%

commit v1 on v0

v1 whole, which is shorter than its diff:
```python
import jax
import jax.numpy as jnp
from jax import lax
from jax.experimental import pallas as pl
from jax.experimental.pallas import tpu as pltpu
from jax.sharding import PartitionSpec as P

HEADS = 12
HEAD_DIM = 64
SLOTS = 4
LANES = 128
BLOCK = 256
NEG = -1e30
f32 = jnp.float32
bf16 = jnp.bfloat16
BOTH = ("dp", "tp")
VM = pl.BlockSpec(memory_space=pltpu.VMEM)
SM = pl.BlockSpec(memory_space=pltpu.SMEM)


def dot_plain(left, right):
    return jnp.dot(left, right, preferred_element_type=f32)


def dot_first(left, right):
    return lax.dot_general(left, right, (((0,), (0,)), ((), ())), preferred_element_type=f32)


def dot_last(left, right):
    return lax.dot_general(left, right, (((1,), (1,)), ((), ())), preferred_element_type=f32)


def unit_of(rows):
    centred = rows - jnp.mean(rows, axis=-1, keepdims=True)
    inv = lax.rsqrt(jnp.mean(centred * centred, axis=-1, keepdims=True) + 1e-06)
    return centred * inv, inv


def unit_back(grad, unit, inv, gain):
    scaled = grad * gain
    inner = (
        scaled
        - jnp.mean(scaled, axis=-1, keepdims=True)
        - unit * jnp.mean(scaled * unit, axis=-1, keepdims=True)
    )
    return inv * inner


def clip_ends(clip_ref):
    ends, total = [], jnp.int32(0)
    for j in range(SLOTS - 1):
        total = total + clip_ref[0, j]
        ends.append(total)
    return ends


def segment_of(position, ends):
    return sum((position >= e).astype(jnp.int32) for e in ends)


def valid_of(start, count, ends):
    position = start + lax.broadcasted_iota(jnp.int32, (count, 1), 0)
    return (position < ends[-1]).astype(f32)


def window_of(low, high, ends, total):
    start, stop = jnp.int32(0), jnp.int32(total)
    for e in ends:
        start = jnp.where(low >= e, e, start)
    for e in ends[::-1]:
        stop = jnp.where(high < e, e, stop)
    block = start // LANES
    return block, (stop + LANES - 1) // LANES - block


def by_width(block, count, total, run):
    most = total // LANES
    widths = [w for w in range(2, most + 1) if w != most - 1]
    before = 0
    for w in widths:

        @pl.when((count > before) & (count <= w))
        def _(w=w):
            run(pl.multiple_of(jnp.minimum(block, most - w) * LANES, LANES), w * LANES)

        before = w


def row_loop(total, size, body):
    def step(i, carry):
        body(pl.multiple_of(i * size, size))
        return carry

    lax.fori_loop(0, total // size, step, 0)


def head_masks(scale):
    lane = lax.broadcasted_iota(jnp.int32, (1, LANES), 1)
    low = lane < HEAD_DIM
    return lane, low, (jnp.where(low, scale, 0.0).astype(bf16), jnp.where(low, 0.0, scale).astype(bf16))


def set_bias(bias_ref, row_start, rows, col_start, cols, ends):
    row_seg = segment_of(row_start + lax.broadcasted_iota(jnp.int32, (rows, 1), 0), ends)
    col_seg = segment_of(col_start + lax.broadcasted_iota(jnp.int32, (1, cols), 1), ends)
    bias_ref[:, :cols] = jnp.where(row_seg == col_seg, 0.0, NEG)


def attend(qkv_ref, ends, mixed_ref, stat_ref, bias_ref):
    total, width = mixed_ref.shape
    lane, low, scaled = head_masks(0.125)

    def block(r0):
        rows = pl.ds(r0, BLOCK)

        def run(k0, cols):
            win = pl.ds(k0, cols)
            set_bias(bias_ref, r0, BLOCK, k0, cols, ends)

            def pair(p, carry):
                c = pl.multiple_of(p * LANES, LANES)
                query = qkv_ref[rows, pl.ds(c, LANES)]
                keys = qkv_ref[win, pl.ds(width + c, LANES)]
                values = qkv_ref[win, pl.ds(2 * width + c, LANES)]
                values = jnp.concatenate([values, jnp.ones_like(values)], axis=1)
                stats, outs = stat_ref[rows, :], []
                for h, mask in enumerate(scaled):
                    scores = dot_last(query * mask, keys) + bias_ref[:, :cols]
                    top = jnp.max(scores, axis=1, keepdims=True)
                    mixed = dot_plain(jnp.exp(scores - top).astype(bf16), values)
                    row_sum = mixed[:, LANES:]
                    outs.append(mixed[:, :LANES] / row_sum)
                    stats = jnp.where(lane == 2 * p + h, top + jnp.log(row_sum), stats)
                stat_ref[rows, :] = stats
                mixed_ref[rows, pl.ds(c, LANES)] = jnp.where(low, outs[0], outs[1]).astype(bf16)
                return carry

            lax.fori_loop(0, width // LANES, pair, 0)

        by_width(*window_of(r0, r0 + BLOCK - 1, ends, total), total, run)

    row_loop(total, BLOCK, block)


def inner_sums(grad_ref, mixed_ref, stat_ref):
    total, width = mixed_ref.shape
    lane, low, _ = head_masks(1.0)

    def block(r0):
        rows = pl.ds(r0, LANES)
        sums = jnp.zeros((LANES, LANES), f32)
        for p in range(width // LANES):
            cols = slice(p * LANES, (p + 1) * LANES)
            both = grad_ref[rows, cols].astype(f32) * mixed_ref[rows, cols].astype(f32)
            first = jnp.sum(jnp.where(low, both, 0.0), axis=1, keepdims=True)
            second = jnp.sum(jnp.where(low, 0.0, both), axis=1, keepdims=True)
            sums = jnp.where(lane == 2 * p, first, jnp.where(lane == 2 * p + 1, second, sums))
        stat_ref[rows, :] = sums

    row_loop(total, LANES, block)


def attend_back(qkv_ref, ends, grad_ref, lse_ref, inner_ref, dqkv_ref, bias_ref, dq_ref):
    total, width = grad_ref.shape
    _, low, scaled = head_masks(0.125)
    _, _, plain = head_masks(1.0)
    dq_ref[...] = jnp.zeros_like(dq_ref)

    def block(r0):
        rows = pl.ds(r0, BLOCK)

        def run(q0, cols):
            win = pl.ds(q0, cols)
            set_bias(bias_ref, r0, BLOCK, q0, cols, ends)

            def pair(p, carry):
                c = pl.multiple_of(p * LANES, LANES)
                keys = qkv_ref[rows, pl.ds(width + c, LANES)]
                values = qkv_ref[rows, pl.ds(2 * width + c, LANES)]
                query = qkv_ref[win, pl.ds(c, LANES)]
                grad = grad_ref[win, pl.ds(c, LANES)]
                dk, dv, dq = [], [], 0.0
                for h in range(2):
                    one = pl.ds(2 * p + h, 1)
                    key = keys * scaled[h]
                    scores = dot_last(key, query) + bias_ref[:, :cols]
                    probs = jnp.exp(scores - lse_ref[one, win])
                    dv.append(dot_plain(probs.astype(bf16), grad))
                    grad_probs = dot_last(values * plain[h], grad)
                    ds = (probs * (grad_probs - inner_ref[one, win])).astype(bf16)
                    dk.append(dot_plain(ds, query))
                    dq = dq + dot_first(ds, key)
                dq_ref[win, pl.ds(c, LANES)] += dq
                dqkv_ref[rows, pl.ds(width + c, LANES)] = (jnp.where(low, dk[0], dk[1]) * 0.125).astype(bf16)
                dqkv_ref[rows, pl.ds(2 * width + c, LANES)] = jnp.where(low, dv[0], dv[1]).astype(bf16)
                return carry

            lax.fori_loop(0, width // LANES, pair, 0)

        by_width(*window_of(r0, r0 + BLOCK - 1, ends, total), total, run)

    row_loop(total, BLOCK, block)
    dqkv_ref[:, :width] = dq_ref[...].astype(bf16)


def set_row(ref, row, value):
    at = lax.broadcasted_iota(jnp.int32, ref.shape, 0) == row
    ref[...] += jnp.where(at, value, 0.0)


def forward_kernel(
    clip_ref, tokens_ref, weights_ref, gains_ref,
    qkv_ref, mixed_ref, lse_ref, middle_ref, feed_ref, normed_ref, sums_ref,
    stat_ref, bias_ref,
):
    total, width = tokens_ref.shape
    ends = clip_ends(clip_ref)
    sums_ref[...] = jnp.zeros_like(sums_ref)

    def norm(r0):
        rows = pl.ds(r0, BLOCK)
        x = tokens_ref[rows, :].astype(f32)
        normed_ref[rows, :] = (unit_of(x)[0] * gains_ref[0:1, :]).astype(bf16)
        set_row(sums_ref, 0, jnp.sum(x * x * valid_of(r0, BLOCK, ends), axis=0, keepdims=True))

    row_loop(total, BLOCK, norm)
    for j in range(3):
        cols = slice(j * width, (j + 1) * width)
        qkv_ref[:, cols] = dot_plain(normed_ref[...], weights_ref[:, cols]).astype(bf16)
    attend(qkv_ref, ends, mixed_ref, stat_ref, bias_ref)
    lse_ref[...] = stat_ref[...].T[: lse_ref.shape[0]]
    middle_ref[...] = dot_plain(mixed_ref[...], weights_ref[:, 3 * width : 4 * width])

    def second(r0):
        rows = pl.ds(r0, BLOCK)
        branch = middle_ref[rows, :]
        middle = tokens_ref[rows, :].astype(f32) + branch
        middle_ref[rows, :] = middle
        feed_ref[rows, :] = (unit_of(middle)[0] * gains_ref[1:2, :]).astype(bf16)
        set_row(sums_ref, 1, jnp.sum(branch * branch * valid_of(r0, BLOCK, ends), axis=0, keepdims=True))

    row_loop(total, BLOCK, second)


def feed_kernel(
    clip_ref, feed_ref, out_grad_ref, middle_ref, gains_ref, weights_ref,
    grads_ref, result_ref, grad_middle_ref, sums_ref,
    grad_ref, active_ref, hidden_ref, out_ref, back_ref,
):
    total, width = feed_ref.shape
    ends = clip_ends(clip_ref)
    step = pl.program_id(0)

    @pl.when(step == 0)
    def _():
        def mask(r0):
            rows = pl.ds(r0, BLOCK)
            grad_ref[rows, :] = (out_grad_ref[rows, :].astype(f32) * valid_of(r0, BLOCK, ends)).astype(bf16)

        row_loop(total, BLOCK, mask)
        out_ref[...] = jnp.zeros_like(out_ref)
        back_ref[...] = jnp.zeros_like(back_ref)
        sums_ref[...] = jnp.zeros_like(sums_ref)

    hid = weights_ref.shape[2] - width
    part = 256
    for n in range(hid // part):
        cols = slice(n * part, (n + 1) * part)
        late = slice(hid + n * part, hid + (n + 1) * part)
        hidden = dot_plain(feed_ref[...], weights_ref[0, :, cols])
        grad_active = dot_plain(grad_ref[...], weights_ref[0, :, late])
        share = 0.5 * (1.0 + lax.erf(hidden * 0.7071067811865476))
        active_ref[:, cols] = (hidden * share).astype(bf16)
        slope = share + hidden * (jnp.exp(-0.5 * hidden * hidden) * 0.3989422804014327)
        hidden_ref[:, cols] = (grad_active * slope).astype(bf16)
    expand, reduce = weights_ref[0, :, :hid], weights_ref[0, :, hid:]
    out_ref[...] += dot_last(active_ref[...], reduce)
    back_ref[...] += dot_last(hidden_ref[...], expand)
    grads_ref[0, :, :hid] = dot_first(feed_ref[...], hidden_ref[...]).astype(bf16)
    grads_ref[0, :, hid:] = dot_first(grad_ref[...], active_ref[...]).astype(bf16)

    @pl.when(step == pl.num_programs(0) - 1)
    def _():
        def finish(r0):
            rows = pl.ds(r0, BLOCK)
            valid = valid_of(r0, BLOCK, ends)
            middle, out, back = middle_ref[rows, :], out_ref[rows, :], back_ref[rows, :]
            result_ref[rows, :] = (middle + out).astype(bf16)
            unit, inv = unit_of(middle)
            grad_middle_ref[rows, :] = (
                grad_ref[rows, :].astype(f32) + unit_back(back, unit, inv, gains_ref[1:2, :])
            )
            set_row(sums_ref, 0, jnp.sum(out * out * valid, axis=0, keepdims=True))
            set_row(sums_ref, 1, jnp.sum(back * unit, axis=0, keepdims=True))

        row_loop(total, BLOCK, finish)


def backward_kernel(
    clip_ref, grad_middle_ref, mixed_ref, qkv_ref, lse_ref, normed_ref, tokens_ref, weights_ref, gains_ref,
    grads_ref, grad_tokens_ref, sums_ref,
    low_ref, grad_ref, dqkv_ref, dq_ref, stat_ref, inner_ref, bias_ref,
):
    total, width = tokens_ref.shape
    ends = clip_ends(clip_ref)
    sums_ref[...] = jnp.zeros_like(sums_ref)
    last = slice(3 * width, 4 * width)
    low_ref[...] = grad_middle_ref[...].astype(bf16)
    grads_ref[:, last] = dot_first(mixed_ref[...], low_ref[...]).astype(bf16)
    grad_ref[...] = dot_last(low_ref[...], weights_ref[:, last]).astype(bf16)
    inner_sums(grad_ref, mixed_ref, stat_ref)
    inner_ref[...] = stat_ref[...].T[: inner_ref.shape[0]]
    attend_back(qkv_ref, ends, grad_ref, lse_ref, inner_ref, dqkv_ref, bias_ref, dq_ref)
    for j in range(3):
        cols = slice(j * width, (j + 1) * width)
        grads_ref[:, cols] = dot_first(normed_ref[...], dqkv_ref[:, cols]).astype(bf16)
    dq_ref[...] = dot_last(dqkv_ref[...], weights_ref[:, : 3 * width])

    def finish(r0):
        rows = pl.ds(r0, BLOCK)
        grad = dq_ref[rows, :]
        unit, inv = unit_of(tokens_ref[rows, :].astype(f32))
        grad_tokens_ref[rows, :] = grad_middle_ref[rows, :] + unit_back(grad, unit, inv, gains_ref[0:1, :])
        set_row(sums_ref, 0, jnp.sum(grad * unit, axis=0, keepdims=True))

    row_loop(total, BLOCK, finish)


def params(**more):
    return pltpu.CompilerParams(vmem_limit_bytes=58 << 20, **more)


def shape(*dims, kind=bf16):
    return jax.ShapeDtypeStruct(dims, kind)


def run_forward(clip, tokens, weights, gains):
    total, width = tokens.shape
    return pl.pallas_call(
        forward_kernel,
        name="layer_forward",
        out_shape=(
            shape(total, 3 * width), shape(total, width), shape(16, total, kind=f32),
            shape(total, width, kind=f32), shape(total, width), shape(total, width), shape(8, width, kind=f32),
        ),
        in_specs=[SM, VM, VM, VM],
        out_specs=(VM,) * 7,
        scratch_shapes=[pltpu.VMEM((total, LANES), f32), pltpu.VMEM((BLOCK, total), f32)],
        compiler_params=params(),
        cost_estimate=pl.CostEstimate(flops=12 * 10**9, bytes_accessed=20 << 20, transcendentals=0),
    )(clip, tokens, weights, gains)


def run_feed(clip, feed, out_grad, middle, gains, weights):
    total, width = feed.shape
    parts, _, both = weights.shape
    one = pl.BlockSpec((1, width, both), lambda t: (t, 0, 0))
    return pl.pallas_call(
        feed_kernel,
        name="feed_both",
        grid=(parts,),
        out_shape=(
            shape(parts, width, both), shape(total, width), shape(total, width, kind=f32), shape(8, width, kind=f32),
        ),
        in_specs=[SM, VM, VM, VM, VM, one],
        out_specs=(one, VM, VM, VM),
        scratch_shapes=[
            pltpu.VMEM((total, width), bf16), pltpu.VMEM((total, both - width), bf16),
            pltpu.VMEM((total, both - width), bf16), pltpu.VMEM((total, width), f32), pltpu.VMEM((total, width), f32),
        ],
        compiler_params=params(),
        cost_estimate=pl.CostEstimate(flops=30 * 10**9, bytes_accessed=30 << 20, transcendentals=0),
    )(clip, feed, out_grad, middle, gains, weights)


def run_backward(clip, grad_middle, mixed, qkv, lse, normed, tokens, weights, gains):
    total, width = tokens.shape
    return pl.pallas_call(
        backward_kernel,
        name="layer_backward",
        out_shape=(shape(width, 4 * width), shape(total, width, kind=f32), shape(8, width, kind=f32)),
        in_specs=[SM] + [VM] * 8,
        out_specs=(VM,) * 3,
        scratch_shapes=[
            pltpu.VMEM((total, width), bf16), pltpu.VMEM((total, width), bf16), pltpu.VMEM((total, 3 * width), bf16),
            pltpu.VMEM((total, width), f32), pltpu.VMEM((total, LANES), f32), pltpu.VMEM((16, total), f32),
            pltpu.VMEM((BLOCK, total), f32),
        ],
        compiler_params=params(),
        cost_estimate=pl.CostEstimate(flops=22 * 10**9, bytes_accessed=30 << 20, transcendentals=0),
    )(clip, grad_middle, mixed, qkv, lse, normed, tokens, weights, gains)


def on_device(
    tokens, clip_lengths, out_grad, w_query, w_key, w_value, w_output, gain_attention, gain_feed, w_expand, w_reduce,
):
    _, total, width = tokens.shape
    rows = tokens.reshape(total, width)
    gain_pair = jnp.stack([gain_attention, gain_feed], axis=1)
    mine = jnp.concatenate([w_query, w_key, w_value, w_output, jnp.pad(gain_pair, ((0, 0), (0, LANES - 2)))], axis=1)
    weights = lax.all_gather(mine, BOTH, axis=0, tiled=True)
    gains = jnp.pad(weights[:, 4 * width : 4 * width + 2].T.astype(f32), ((0, 6), (0, 0)))
    hid = w_expand.shape[1]
    both = jnp.concatenate([w_expand, w_reduce.T], axis=1)
    feed_weights = lax.all_gather(both, ("tp", "dp"), axis=0, tiled=True).reshape(-1, width, both.shape[1])

    qkv, mixed, lse, middle, feed, normed, sums_one = run_forward(clip_lengths, rows, weights, gains)
    feed_grads, result, grad_middle, sums_two = run_feed(
        clip_lengths, feed, out_grad.reshape(total, width), middle, gains, feed_weights
    )
    shard_feed = lax.psum_scatter(
        feed_grads.reshape(-1, feed_grads.shape[-1]), ("tp", "dp"), scatter_dimension=0, tiled=True
    )
    grads, grad_tokens, sums_three = run_backward(
        clip_lengths, grad_middle, mixed, qkv, lse, normed, rows, weights, gains
    )
    shard = lax.psum_scatter(grads, BOTH, scatter_dimension=0, tiled=True).astype(f32)
    count = jnp.sum(clip_lengths[:, : SLOTS - 1]).astype(f32)
    squares = [jnp.sum(sums_one[0]), jnp.sum(sums_one[1]), jnp.sum(sums_two[0]), count]
    small = jnp.concatenate([sums_three[0], sums_two[1], jnp.stack(squares)])
    small = lax.psum(small, BOTH)
    gain_grads = lax.dynamic_slice_in_dim(
        small[: 2 * width].reshape(2, width), lax.axis_index(BOTH) * gain_feed.shape[0], gain_feed.shape[0], axis=1
    )
    stats = small[2 * width :]
    means = jnp.sqrt(stats[:3] / (stats[3] * width))
    shard_feed = shard_feed.astype(f32)
    return (
        result.reshape(1, total, width),
        grad_tokens.reshape(1, total, width),
        shard[:, :width],
        shard[:, width : 2 * width],
        shard[:, 2 * width : 3 * width],
        shard[:, 3 * width :],
        gain_grads[0],
        gain_grads[1],
        shard_feed[:, :hid],
        shard_feed[:, hid:].T,
        means,
    )


def solution(mesh):
    row, flat = P(BOTH, None), P(BOTH)
    whole = P(BOTH, None, None)
    in_specs = (whole, row, whole, row, row, row, row, flat, flat, P("dp", "tp"), P("tp", "dp"))
    out_specs = (whole, whole, row, row, row, row, flat, flat, P("dp", "tp"), P("tp", "dp"), P())
    return jax.shard_map(on_device, mesh=mesh, in_specs=in_specs, out_specs=out_specs, check_vma=False)
```

time: 1270 us -> 519 us (0.41)
  waiting for transfers between devices: 746 us -> 311 us
  matrix products: 299 us -> 0 us
  Pallas kernels: 0 us -> 128 us
  other arithmetic: 57.1 us -> 8.06 us
  local copies, waits for them, and re-layouts: 57.7 us -> 12.9 us
  blocking collectives: 81.8 us -> 42.6 us
    dot_general x102 -> x0, matrix products: 299 us -> none  [the longest x42 128 us: dot_last(): lax.dot_general(left_side, right_side, (((1,), (1,)), ((), ())), preferre...]
    reduce_scatter x8 -> x2, waiting for transfers between devices: 491 us -> 197 us  [the longest x1 140 us: on_device(): lax.psum_scatter(feed_grads.reshape(-1, feed_grads.shape[-1]), ('tp', 'dp...]
    all_gather x8 -> x2, waiting for transfers between devices: 251 us -> 114 us  [the longest x1 65.4 us: on_device(): weights = lax.all_gather(mine, BOTH, axis=0, tiled=True)]
    pallas_call x0 -> x3, Pallas kernels: none -> 128 us  [the longest x1 53.2 us: run_backward(): pl.pallas_call(backward_kernel, name='layer_backward', out_shape=(shape(w...]
    unnamed x2 -> x0, blocking collectives: 81.8 us -> none
    psum x0 -> x1, blocking collectives: none -> 42.6 us  [on_device(): small = lax.psum(small, BOTH)]
    convert_element_type x18 -> x1, other arithmetic: 28.1 us -> 1.01 us  [on_device(): shard_feed = shard_feed.astype(f32)]
    reduce_sum x19 -> x3, other arithmetic: 23.8 us -> 3.48 us  [the longest x1 1.43 us: on_device(): jnp.sum(sums_one[1])]
  transfers between devices with their start and end apart: 16 -> 4, of which waited for: 13 -> 4; matrix products, arithmetic and copies ran while one was open for 29% -> 2% of each run, Pallas kernels for 0% -> 7%
where the time goes in v1:
time: 519 us; the launch traced here: 518 us
  waiting for transfers between devices  311 us (60%)
  Pallas kernels  128 us (25%)
  blocking collectives  42.6 us (8%)
  between operations  15.1 us (3%)
  local copies, waits for them, and re-layouts  12.9 us (2%)
  other arithmetic  8.06 us (2%)
    reduce_scatter x1, waiting for transfers between devices, on_device(): lax.psum_scatter(feed_grads.reshape(-1, feed_grads.shape[-1]), ('tp', 'dp...  140 us
    all_gather x1, waiting for transfers between devices, on_device(): weights = lax.all_gather(mine, BOTH, axis=0, tiled=True)  65.4 us
    reduce_scatter x1, waiting for transfers between devices, on_device(): lax.psum_scatter(grads, BOTH, scatter_dimension=0, tiled=True).astype(f32)  56.5 us
    pallas_call x1, Pallas kernels, run_backward(): pl.pallas_call(backward_kernel, name='layer_backward', out_shape=(shape(w...  53.2 us
    all_gather x1, waiting for transfers between devices, on_device(): lax.all_gather(both, ('tp', 'dp'), axis=0, tiled=True)  48.9 us
    psum x1, blocking collectives, on_device(): small = lax.psum(small, BOTH)  42.6 us
    pallas_call x1, Pallas kernels, run_feed(): pl.pallas_call(feed_kernel, name='feed_both', grid=(parts,), out_shape=(s...  41.1 us
    pallas_call x1, Pallas kernels, run_forward(): pl.pallas_call(forward_kernel, name='layer_forward', out_shape=(shape(tot...  33.9 us
  transfers between devices with their start and end apart: 4, of which 4 were waited for; matrix products, arithmetic and copies ran while one was open for 2% of the time, Pallas kernels for 7%

profile of v1, /device:TPU:0, one launch (start us, length us, event | category | flops | bytes accessed | tf_op | source)
XLA Modules:
  0.0 518.3 jit_solution(5064661708681448669)
XLA Ops:
  7.2 0.7 pad_maximum_fusion.1
  8.0 0.8 constant_dynamic-update-slice_fusion.4
  8.8 0.8 constant_dynamic-update-slice_fusion.3
  9.5 0.8 constant_dynamic-update-slice_fusion.2
  10.3 0.8 constant_dynamic-update-slice_fusion.1
  11.1 0.7 copy-done
  11.8 1.7 pad_maximum_fusion
  13.6 65.4 %all-gather.3.cloned.1.call-done.weights_ref = bf16[768,3200]{1,0:T(8,128)(2,1)} async-done(((bf16[24,3200]{1,0:T(8,128)(2,1)}), bf16[768,3200]{1,0:T(8,128)(2,1)}) %all-gather.3.cloned.1.call-update) | async-done | bytes 4915216 | tf_op jit(solution)/shard_map/all_gather | solution.py:401
  79.0 0.9 slice.75
  80.0 0.1 copy.30
  80.1 0.6 pad_convert_fusion.gains_ref
  80.7 33.9 %layer_forward.1 = (bf16[1024,2304]{1,0:T(8,128)(2,1)}, bf16[1024,768]{1,0:T(8,128)(2,1)}, f32[16,1024]{1,0:T(8,128)}, f32[1024,768]{1,0:T(8,128)}, bf16[1024,76...) custom-call(s32[1,4]{1,0:T(1,128)} %clip_ref.5, bf16[1024,768]{1,0:T(8,128)(2,1)} %bitcast.28, ...), custom_call_target="tpu_custom_call" | custom-call | flops 12000000000 | bytes 20971520 | tf_op jit(solution)/shard_map/layer_forward/pallas_call | solution.py:339
  114.6 48.9 %all-gather.5.cloned.1.call-done = bf16[3072,1536]{1,0:T(8,128)(2,1)} async-done(((bf16[96,1536]{1,0:T(8,128)(2,1)}), bf16[3072,1536]{1,0:T(8,128)(2,1)}) %all-gather.5.cloned.1.call-update) | async-done | bytes 9437200 | tf_op jit(solution)/shard_map/all_gather | solution.py:405
  163.5 41.1 %feed_both.1 = (bf16[4,768,1536]{2,1,0:T(8,128)(2,1)}, bf16[1024,768]{1,0:T(8,128)(2,1)}, f32[1024,768]{1,0:T(8,128)}, f32[8,768]{1,0:T(8,128)}) custom-call(s32[1,4]{1,0:T(1,128)} %clip_ref.5, bf16[1024,768]{1,0:T(8,128)(2,1)} %get-tuple-element.25.feed_ref, bf16[1024,768]{1,0:T(8,128)(2,1)} %bitcast.27, f32[1024,768]{1,0:T(8,128)} %get-tuple-element.26.middle_ref, ...), custom_call_target="tpu_custom_call" | custom-call | flops 30000001024 | bytes 31457280 | tf_op jit(solution)/shard_map/feed_both/pallas_call | solution.py:358
  204.6 53.2 %layer_backward.1 = (bf16[768,3072]{1,0:T(8,128)(2,1)}, f32[1024,768]{1,0:T(8,128)}, f32[8,768]{1,0:T(8,128)}) custom-call(s32[1,4]{1,0:T(1,128)} %clip_ref.5, f32[1024,768]{1,0:T(8,128)} %get-tuple-element.28.grad_middle_ref, bf16[1024,768]{1,0:T(8,128)(2,1)} %get-tuple-element.29.mixed_ref, bf16[1024,2304]{1,0:T(8,128)(2,1)} %get-tuple-element.30.qkv_ref, ...), custom_call_target="tpu_custom_call" | custom-call | flops 22000001024 | bytes 31457280 | tf_op jit(solution)/shard_map/layer_backward/pallas_call | solution.py:378
  257.8 0.5 reduce-scatter.5.cloned.1.call-update
  258.4 0.1 copy-done.1
  258.5 0.6 slice_reduce_fusion.5
  259.8 1.4 slice_reduce_fusion.1
  261.2 0.8 slice_reduce_fusion.4
  261.9 1.4 slice_reduce_fusion
  263.4 2.0 concatenate.11
  265.4 42.6 %psum.7 = f32[1540]{0:T(1024)S(1)} all-reduce(f32[1540]{0:T(1024)S(1)} %concatenate.11), channel_id=1, replica_groups=mesh['dp'=8,'tp'=4] {'dp','tp'}, use_global_device_ids=true, to_apply=%region_5.6 | all-reduce | flops 1540 | bytes 12320 | tf_op jit(solution)/shard_map/psum | solution.py:421
  308.0 0.6 slice.84
  309.3 0.5 slice_bitcast_fusion.1
  309.9 0.5 fusion
  310.4 56.5 %reduce-scatter.3.cloned.1.call-done = bf16[24,3072]{1,0:T(8,128)(2,1)} async-done(((bf16[768,3072]{1,0:T(8,128)(2,1)}), bf16[24,3072]{1,0:T(8,128)(2,1)}) %reduce-scatter.3.cloned.1.call-update) | async-done | bytes 147472 | tf_op jit(solution)/shard_map/reduce_scatter | solution.py:417
  366.9 1.5 fusion.1
  368.4 140.0 %reduce-scatter.5.cloned.1.call-done = bf16[96,1536]{1,0:T(8,128)(2,1)} async-done(((bf16[3072,1536]{1,0:T(8,128)(2,1)}), bf16[96,1536]{1,0:T(8,128)(2,1)}) %reduce-scatter.5.cloned.1.call-update) | async-done | bytes 294928 | tf_op jit(solution)/shard_map/reduce_scatter | solution.py:411
  508.4 1.0 convert_element_type.20
  509.4 0.7 slice_bitcast_fusion
  510.2 1.6 slice.81
  (13 shorter events, 0.4 us)
Async XLA Ops:
  7.2 71.8 %all-gather.3.cloned.1.call-start = ((), (), s32[]{:S(2)}) async-start(), calls=%async_computation.2 | async-start | bytes 5068800 | tf_op jit(solution)/shard_map/all_gather | solution.py:401
  11.1 0.7 copy-start
  11.8 151.7 %all-gather.5.cloned.1.call-start = ((), (), s32[]{:S(2)}) async-start(), calls=%async_computation.3 | async-start | bytes 9732096 | tf_op jit(solution)/shard_map/all_gather | solution.py:405
  13.6 353.3 %reduce-scatter.3.cloned.1.call-start = ((), (), s32[]{:S(2)}) async-start(), calls=%async_computation.4 | async-start | bytes 4866048 | tf_op jit(solution)/shard_map/reduce_scatter | solution.py:417
  257.8 250.6 %reduce-scatter.5.cloned.1.call-start = ((), (), s32[]{:S(2)}) async-start(), calls=%async_computation.5 | async-start | bytes 9732096 | tf_op jit(solution)/shard_map/reduce_scatter | solution.py:411
  257.8 0.7 copy-start.1
Sparse Core Ops, SparseCore 0:
  11.9 67.0 all-gather.2
  82.5 80.9 all-gather.4
  257.9 108.9 reduce-scatter.2
  373.7 134.7 reduce-scatter.4

commit v2 on v1

--- a/solution.py
+++ b/solution.py
@@ -391,19 +391,219 @@
     )(clip, grad_middle, mixed, qkv, lse, normed, tokens, weights, gains)
 
 
+MESH = pl.DeviceIdType.MESH
+ANY = pl.BlockSpec(memory_space=pl.ANY)
+FACTORS = {
+    (8, 4): ((("z", 4), ("y", 2)), (("x", 2), ("c", 2))),
+    (64, 4): ((("y", 4), ("z", 8), ("c", 2)), (("x", 4),)),
+}
+
+
+class Net:
+    def __init__(self, factors):
+        self.factors = factors
+        self.size = {n: s for axis in factors for n, s in axis}
+
+    def locate(self):
+        self.place = {}
+        for name, axis in zip(BOTH, self.factors):
+            left = lax.axis_index(name)
+            for n, s in axis[::-1]:
+                self.place[n] = lax.rem(left, s)
+                left = lax.div(left, s)
+
+    def device(self, dim, value):
+        out = []
+        for axis in self.factors:
+            index = 0
+            for n, s in axis:
+                index = index * s + (value if n == dim else self.place[n])
+            out.append(index)
+        return tuple(out)
+
+    def names(self, order):
+        axes = dict(zip(BOTH, self.factors))
+        return [n for a in order for n, _ in axes[a]]
+
+    def dims(self, order):
+        return tuple(self.size[n] for n in self.names(order))
+
+    def view(self, ref, order, lanes, **fixed):
+        index = tuple(fixed.get(n, slice(None)) for n in self.names(order))
+        return ref.at[index + (slice(None), pl.ds(*lanes))]
+
+    def peers(self, dim):
+        s = self.size[dim]
+        return [lax.rem(self.place[dim] + o, s) for o in range(1, s)]
+
+    def enter(self):
+        barrier, count = pltpu.get_barrier_semaphore(), 0
+        for dim in self.size:
+            for v in self.peers(dim):
+                pl.semaphore_signal(barrier, inc=1, device_id=self.device(dim, v), device_id_type=MESH)
+                count += 1
+        pl.semaphore_wait(barrier, count)
+
+
+class Sems:
+    def __init__(self, send, recv):
+        self.send, self.recv, self.used = send, recv, 0
+
+    def take(self):
+        self.used += 1
+        return self.send.at[self.used - 1], self.recv.at[self.used - 1]
+
+
+def spread(net, sems, dim, source, target):
+    out = []
+    for v in net.peers(dim):
+        send, recv = sems.take()
+        copy = pltpu.make_async_remote_copy(
+            src_ref=source, dst_ref=target, send_sem=send, recv_sem=recv,
+            device_id=net.device(dim, v), device_id_type=MESH,
+        )
+        copy.start()
+        out.append(copy)
+    return out
+
+
+def arrive(copies):
+    for copy in copies:
+        copy.wait_recv()
+
+
+class Piece:
+    def __init__(self, net, sems, mine, ref, order, lanes, first, second):
+        self.net, self.sems, self.mine, self.ref, self.order, self.lanes = net, sems, mine, ref, order, lanes
+        self.first, self.second, self.sent, self.twin = first, second, [], []
+
+    def block(self, free, **other):
+        fixed = {n: v for n, v in self.net.place.items() if n not in free}
+        return self.net.view(self.ref, self.order, self.lanes, **{**fixed, **other})
+
+    def pass_on(self, dim, block, source=None):
+        copies = spread(self.net, self.sems, dim, block if source is None else source, block)
+        self.sent += copies
+        return copies
+
+    def start(self):
+        self.z = self.pass_on("z", self.block(()), self.mine.at[:, pl.ds(*self.lanes)])
+
+    def step_one(self):
+        arrive(self.z)
+        self.one = self.pass_on(self.first, self.block(("z",)))
+        self.twin += self.pass_on("c", self.block(("z",)))
+
+    def step_two(self):
+        arrive(self.one)
+        self.two = self.pass_on(self.second, self.block(("z", self.first)))
+        for v in self.net.peers(self.first):
+            self.twin += self.pass_on("c", self.block(("z",), **{self.first: v}))
+
+    def step_three(self):
+        arrive(self.two)
+        for v in self.net.peers(self.second):
+            self.twin += self.pass_on("c", self.block(("z", self.first), **{self.second: v}))
+
+    def ready(self):
+        arrive(self.twin)
+
+    def drain(self):
+        for copy in self.sent:
+            copy.wait_send()
+
+
+def copies_of(net):
+    z, y, x, c = (net.size[n] - 1 for n in "zyxc")
+    return z + y + x + c * (1 + y + x)
+
+
+def lane_parts(width, count):
+    tiles, out, at = width // LANES, [], 0
+    for i in range(count):
+        take = (tiles - at) // (count - i)
+        out.append((at * LANES, take * LANES))
+        at += take
+    return out
+
+
+ORDERS = (("y", "x"), ("x", "y"))
+ATT_PARTS = 4
+FEED_PARTS = 4
+
+
+def gather_kernel(net, att_ref, feed_ref, att_all, feed_all, send, recv, local):
+    net.locate()
+    net.enter()
+    sems = Sems(send, recv)
+    flip = BOTH[::-1]
+    att = [
+        Piece(net, sems, att_ref, att_all, BOTH, lanes, *ORDERS[i % 2])
+        for i, lanes in enumerate(lane_parts(att_ref.shape[1], ATT_PARTS))
+    ]
+    feed = [
+        Piece(net, sems, feed_ref, feed_all, flip, lanes, *ORDERS[i % 2])
+        for i, lanes in enumerate(lane_parts(feed_ref.shape[1], FEED_PARTS))
+    ]
+    own = [
+        pltpu.make_async_copy(att_ref, net.view(att_all, BOTH, (0, att_ref.shape[1]), **net.place), local.at[0]),
+        pltpu.make_async_copy(feed_ref, net.view(feed_all, flip, (0, feed_ref.shape[1]), **net.place), local.at[1]),
+    ]
+    for copy in own:
+        copy.start()
+    for p in att:
+        p.start()
+    for copy in own:
+        copy.wait()
+    for p in att:
+        p.step_one()
+    for p in feed:
+        p.start()
+    for p in att:
+        p.step_two()
+    for p in att:
+        p.step_three()
+    for p in feed:
+        p.step_one()
+    for p in feed:
+        p.step_two()
+    for p in feed:
+        p.step_three()
+    for p in att + feed:
+        p.ready()
+    for p in att + feed:
+        p.drain()
+
+
+def run_gather(net, att, feed):
+    count = (ATT_PARTS + FEED_PARTS) * copies_of(net)
+    return pl.pallas_call(
+        lambda *refs: gather_kernel(net, *refs),
+        name="gather_weights",
+        out_shape=(shape(*net.dims(BOTH), *att.shape), shape(*net.dims(BOTH[::-1]), *feed.shape)),
+        in_specs=[ANY, ANY],
+        out_specs=(ANY, ANY),
+        scratch_shapes=[
+            pltpu.SemaphoreType.DMA((count,)), pltpu.SemaphoreType.DMA((count,)), pltpu.SemaphoreType.DMA((2,)),
+        ],
+        compiler_params=pltpu.CompilerParams(collective_id=1, has_side_effects=True),
+    )(att, feed)
+
+
 def on_device(
+    net,
     tokens, clip_lengths, out_grad, w_query, w_key, w_value, w_output, gain_attention, gain_feed, w_expand, w_reduce,
 ):
     _, total, width = tokens.shape
     rows = tokens.reshape(total, width)
     gain_pair = jnp.stack([gain_attention, gain_feed], axis=1)
     mine = jnp.concatenate([w_query, w_key, w_value, w_output, jnp.pad(gain_pair, ((0, 0), (0, LANES - 2)))], axis=1)
-    weights = lax.all_gather(mine, BOTH, axis=0, tiled=True)
-    gains = jnp.pad(weights[:, 4 * width : 4 * width + 2].T.astype(f32), ((0, 6), (0, 0)))
     hid = w_expand.shape[1]
     both = jnp.concatenate([w_expand, w_reduce.T], axis=1)
-    feed_weights = lax.all_gather(both, ("tp", "dp"), axis=0, tiled=True).reshape(-1, width, both.shape[1])
-
+    weights, feed_weights = run_gather(net, mine, both)
+    weights = weights.reshape(width, -1)
+    feed_weights = feed_weights.reshape(-1, width, both.shape[1])
+    gains = jnp.pad(weights[:, 4 * width : 4 * width + 2].T.astype(f32), ((0, 6), (0, 0)))
     qkv, mixed, lse, middle, feed, normed, sums_one = run_forward(clip_lengths, rows, weights, gains)
     feed_grads, result, grad_middle, sums_two = run_feed(
         clip_lengths, feed, out_grad.reshape(total, width), middle, gains, feed_weights
@@ -445,4 +645,5 @@
     whole = P(BOTH, None, None)
     in_specs = (whole, row, whole, row, row, row, row, flat, flat, P("dp", "tp"), P("tp", "dp"))
     out_specs = (whole, whole, row, row, row, row, flat, flat, P("dp", "tp"), P("tp", "dp"), P())
-    return jax.shard_map(on_device, mesh=mesh, in_specs=in_specs, out_specs=out_specs, check_vma=False)
+    net = Net(FACTORS[mesh.shape["dp"], mesh.shape["tp"]])
+    return jax.shard_map(lambda *args: on_device(net, *args), mesh=mesh, in_specs=in_specs, out_specs=out_specs, check_vma=False)

time: 519 us -> 491 us (0.946)
  waiting for transfers between devices: 311 us -> 197 us
  Pallas kernels: 128 us -> 215 us
    all_gather x2 -> x0, waiting for transfers between devices: 114 us -> none  [the longest x1 65.4 us: on_device(): weights = lax.all_gather(mine, BOTH, axis=0, tiled=True)]
    pallas_call x0 -> x1, Pallas kernels: none -> 85.5 us  [run_gather(): pl.pallas_call(lambda *refs: gather_kernel(net, *refs), name='gather_weig...]
  transfers between devices with their start and end apart: 4 -> 2, of which waited for: 4 -> 2; matrix products, arithmetic and copies ran while one was open for 2% -> 2% of each run, Pallas kernels for 7% -> 0%
where the time goes in v2:
time: 491 us; the launch traced here: 490 us
  Pallas kernels  215 us (44%)
  waiting for transfers between devices  197 us (40%)
  blocking collectives  41.5 us (8%)
  between operations  15.4 us (3%)
  local copies, waits for them, and re-layouts  12.1 us (2%)
  other arithmetic  8.11 us (2%)
    reduce_scatter x1, waiting for transfers between devices, on_device(): lax.psum_scatter(feed_grads.reshape(-1, feed_grads.shape[-1]), ('tp', 'dp...  140 us
    pallas_call x1, Pallas kernels, run_gather(): pl.pallas_call(lambda *refs: gather_kernel(net, *refs), name='gather_weig...  85.5 us
    reduce_scatter x1, waiting for transfers between devices, on_device(): lax.psum_scatter(grads, BOTH, scatter_dimension=0, tiled=True).astype(f32)  56.1 us
    pallas_call x1, Pallas kernels, run_backward(): pl.pallas_call(backward_kernel, name='layer_backward', out_shape=(shape(w...  54 us
    psum x1, blocking collectives, on_device(): small = lax.psum(small, BOTH)  41.5 us
    pallas_call x1, Pallas kernels, run_feed(): pl.pallas_call(feed_kernel, name='feed_both', grid=(parts,), out_shape=(s...  41.3 us
    pallas_call x1, Pallas kernels, run_forward(): pl.pallas_call(forward_kernel, name='layer_forward', out_shape=(shape(tot...  34.5 us
  transfers between devices with their start and end apart: 2, of which 2 were waited for; matrix products, arithmetic and copies ran while one was open for 2% of the time, Pallas kernels for 0%

profile of v2, /device:TPU:0, one launch (start us, length us, event | category | flops | bytes accessed | tf_op | source)
XLA Modules:
  0.0 489.6 jit_solution(9202317115480913504)
XLA Ops:
  7.2 0.7 pad_maximum_fusion.1
  7.9 0.1 copy.30
  8.0 0.8 constant_dynamic-update-slice_fusion.4
  8.8 0.8 constant_dynamic-update-slice_fusion.3
  9.5 0.8 constant_dynamic-update-slice_fusion.2
  10.3 0.8 constant_dynamic-update-slice_fusion.1
  11.1 1.8 pad_maximum_fusion.refs_1_
  12.9 85.5 %gather_weights.1 = (bf16[4,2,2,2,24,3200]{5,4,3,2,1,0:T(8,128)(2,1)}, bf16[2,2,4,2,96,1536]{5,4,3,2,1,0:T(8,128)(2,1)}) custom-call(bf16[24,3200]{1,0:T(8,128)(2,1)} %copy-done, bf16[96,1536]{1,0:T(8,128)(2,1)} %pad_maximum_fusion.refs_1_), custom_call_target="tpu_custom_call" | custom-call | tf_op jit(solution)/shard_map/gather_weights/pallas_call | solution.py:580
  98.4 0.9 slice.75
  99.4 0.1 copy.32
  99.5 0.6 pad_convert_fusion.gains_ref
  100.1 34.5 %layer_forward.1 = (bf16[1024,2304]{1,0:T(8,128)(2,1)}, bf16[1024,768]{1,0:T(8,128)(2,1)}, f32[16,1024]{1,0:T(8,128)}, f32[1024,768]{1,0:T(8,128)}, bf16[1024,76...) custom-call(s32[1,4]{1,0:T(1,128)} %clip_ref.5, bf16[1024,768]{1,0:T(8,128)(2,1)} %bitcast.32, ...), custom_call_target="tpu_custom_call" | custom-call | flops 12000000000 | bytes 20971520 | tf_op jit(solution)/shard_map/layer_forward/pallas_call | solution.py:339
  134.6 41.3 %feed_both.1 = (bf16[4,768,1536]{2,1,0:T(8,128)(2,1)}, bf16[1024,768]{1,0:T(8,128)(2,1)}, f32[1024,768]{1,0:T(8,128)}, f32[8,768]{1,0:T(8,128)}) custom-call(s32[1,4]{1,0:T(1,128)} %clip_ref.5, bf16[1024,768]{1,0:T(8,128)(2,1)} %get-tuple-element.28.feed_ref, bf16[1024,768]{1,0:T(8,128)(2,1)} %bitcast.31, f32[1024,768]{1,0:T(8,128)} %get-tuple-element.29.middle_ref, ...), custom_call_target="tpu_custom_call" | custom-call | flops 30000001024 | bytes 31457280 | tf_op jit(solution)/shard_map/feed_both/pallas_call | solution.py:358
  175.9 54.0 %layer_backward.1 = (bf16[768,3072]{1,0:T(8,128)(2,1)}, f32[1024,768]{1,0:T(8,128)}, f32[8,768]{1,0:T(8,128)}) custom-call(s32[1,4]{1,0:T(1,128)} %clip_ref.5, f32[1024,768]{1,0:T(8,128)} %get-tuple-element.32.grad_middle_ref, bf16[1024,768]{1,0:T(8,128)(2,1)} %get-tuple-element.33.mixed_ref, bf16[1024,2304]{1,0:T(8,128)(2,1)} %get-tuple-element.34.qkv_ref, ...), custom_call_target="tpu_custom_call" | custom-call | flops 22000001024 | bytes 31457280 | tf_op jit(solution)/shard_map/layer_backward/pallas_call | solution.py:378
  229.9 0.0 reduce-scatter.5.cloned.1.call-start
  230.0 0.7 reduce-scatter.5.cloned.1.call-update
  230.7 0.6 slice_reduce_fusion.5
  232.0 0.8 slice_reduce_fusion.4
  232.7 1.4 slice_reduce_fusion.1
  234.2 1.4 slice_reduce_fusion
  235.6 2.0 concatenate.11
  237.6 41.5 %psum.7 = f32[1540]{0:T(1024)S(1)} all-reduce(f32[1540]{0:T(1024)S(1)} %concatenate.11), channel_id=1, replica_groups=mesh['dp'=8,'tp'=4] {'dp','tp'}, use_global_device_ids=true, to_apply=%region_5.6 | all-reduce | flops 1540 | bytes 12320 | tf_op jit(solution)/shard_map/psum | solution.py:621
  279.2 0.6 slice.84
  280.4 0.1 constant_dynamic-slice_fusion
  280.5 0.5 slice_bitcast_fusion.1
  281.0 0.5 fusion
  281.5 56.1 %reduce-scatter.3.cloned.1.call-done = bf16[24,3072]{1,0:T(8,128)(2,1)} async-done(((bf16[768,3072]{1,0:T(8,128)(2,1)}), bf16[24,3072]{1,0:T(8,128)(2,1)}) %reduce-scatter.3.cloned.1.call-update) | async-done | bytes 147472 | tf_op jit(solution)/shard_map/reduce_scatter | solution.py:617
  337.7 1.5 fusion.1
  339.2 140.2 %reduce-scatter.5.cloned.1.call-done = bf16[96,1536]{1,0:T(8,128)(2,1)} async-done(((bf16[3072,1536]{1,0:T(8,128)(2,1)}), bf16[96,1536]{1,0:T(8,128)(2,1)}) %reduce-scatter.5.cloned.1.call-update) | async-done | bytes 294928 | tf_op jit(solution)/shard_map/reduce_scatter | solution.py:611
  479.4 1.0 convert_element_type.20
  480.4 0.7 slice_bitcast_fusion
  481.1 1.6 slice.81
  (8 shorter events, 0.1 us)
Async XLA Ops:
  7.2 330.5 %reduce-scatter.3.cloned.1.call-start = ((), (), s32[]{:S(2)}) async-start(), calls=%async_computation.2 | async-start | bytes 4866048 | tf_op jit(solution)/shard_map/reduce_scatter | solution.py:617
  11.1 1.8 copy-start
  229.9 249.4 %reduce-scatter.5.cloned.1.call-start = ((), (), s32[]{:S(2)}) async-start(), calls=%async_computation.3 | async-start | bytes 9732096 | tf_op jit(solution)/shard_map/reduce_scatter | solution.py:611
  230.0 0.7 copy-start.1
Sparse Core Ops, SparseCore 0:
  230.1 107.5 reduce-scatter.2
  344.6 134.7 reduce-scatter.4
